TPU v7x, 128 devices: a whole 4x4x4 slice. The times are simulated.
128 devices in a mesh: gx: 16 (over y, z_lo, core), gy: 8 (over x, z_hi).
Axes of the slice: x: 4, y: 4, z: 4 (z_hi: 2, z_lo: 2; z = z_hi * 2 + z_lo), core: 2. Of those that a mesh axis runs over, the one named last changes fastest.
Arguments:
- populations: float32 [19, 256, 256, 128], P(None, 'gx', 'gy'), may hold values from 0 to 10, as said below
- solid: int32 [256, 256, 128], P('gx', 'gy'), may hold values 0 or 1
Outputs:
- advanced: float32 [19, 256, 256, 128], P(None, 'gx', 'gy')
Inputs may be any that keep to these rules, and one draw needn't show every extreme that they name: populations are positive, each between 0.5 w_i 18 and 1.5 w_i 18.
All inputs are finite; a program needn't handle non-finite values. No bound on the sum of `solid` on one device may be relied on, other than what follows from the above.
Results may differ from a plain program's by a relative error of at most 0.0001.
Values sent between devices are 32-bit elements; how exact they have to be, the bound alone decides.
No kernel may reach another device: no remote copies, remote signals or barrier semaphores. Data moves between devices by JAX's collectives and lax.ppermute only.
A program may use at most 128 MiB of HBM per device.

v0:
```python
import jax
import jax.numpy as jnp
from jax import lax
from jax.experimental import pallas as pl
from jax.experimental.pallas import tpu as pltpu
from jax.sharding import PartitionSpec as P


ITERS = 3
NQ = 19
VEL = (
    (0, 0, 0),
    (1, 0, 0), (-1, 0, 0), (0, 1, 0), (0, -1, 0), (0, 0, 1), (0, 0, -1),
    (1, 1, 0), (-1, -1, 0), (1, -1, 0), (-1, 1, 0),
    (1, 0, 1), (-1, 0, -1), (1, 0, -1), (-1, 0, 1),
    (0, 1, 1), (0, -1, -1), (0, 1, -1), (0, -1, 1),
)
RELAX = 1.6
XP = tuple(i for i in range(NQ) if VEL[i][0] == 1)
XM = tuple(i for i in range(NQ) if VEL[i][0] == -1)
YP = tuple(i for i in range(NQ) if VEL[i][1] == 1)
YM = tuple(i for i in range(NQ) if VEL[i][1] == -1)
MARK = -float(2 ** 20)
EDGE = -1e5


def opposite(i):
    if i == 0:
        return 0
    return i + 1 if i % 2 == 1 else i - 1


def collide(f):
    keep = 1.0 - RELAX
    d = {i: f[i] - f[i + 1] for i in range(1, NQ, 2)}
    s = [f[i] + f[i + 1] for i in range(1, NQ, 2)]
    rho = ((s[0] + s[1]) + (s[2] + s[3])) + ((s[4] + s[5]) + (s[6] + s[7])) + (s[8] + f[0])
    mx = (d[1] + d[7]) + (d[9] + d[11]) + d[13]
    my = (d[3] + d[7]) + (d[15] - d[9]) + d[17]
    mz = (d[5] + d[11]) + (d[15] - d[13]) - d[17]
    inv = 1.0 / rho
    ux, uy, uz = mx * inv, my * inv, mz * inv
    a, b, c = mx * ux, my * uy, mz * uz
    base = rho - 1.5 * ((a + b) + c)
    w0, w1, w2 = RELAX / 3.0, RELAX / 18.0, RELAX / 36.0
    post = [None] * NQ
    post[0] = keep * f[0] + w0 * base
    one, two = w1 * base, w2 * base

    def pair(i, even, odd):
        post[i] = keep * f[i] + (even + odd)
        post[i + 1] = keep * f[i + 1] + (even - odd)

    k1, o1 = 4.5 * w1, 3.0 * w1
    pair(1, one + k1 * a, o1 * mx)
    pair(3, one + k1 * b, o1 * my)
    pair(5, one + k1 * c, o1 * mz)
    k2, o2 = 4.5 * w2, 3.0 * w2
    qx, qy, qz = o2 * mx, o2 * my, o2 * mz
    ka, kb, kc = k2 * a, k2 * b, k2 * c
    kx, ky = (2.0 * k2) * mx, (2.0 * k2) * my
    for i, even, cross, p, q in (
        (7, two + (ka + kb), kx * uy, qx, qy),
        (11, two + (ka + kc), kx * uz, qx, qz),
        (15, two + (kb + kc), ky * uz, qy, qz),
    ):
        pair(i, even + cross, p + q)
        pair(i + 2, even - cross, p - q)
    return post


def send_faces(x, t, last_x, last_t, raw, xp, xm, yp, ym):
    fixed = isinstance(x, int)
    rows = pl.ds(8 * t, 8)
    if fixed and x == last_x:
        for k, v in enumerate(raw(XP)):
            xp[k, rows, :] = v
    if fixed and x == 0:
        for k, v in enumerate(raw(XM)):
            xm[k, rows, :] = v
    for side, ref, group, row in ((last_t, yp, YP, 7), (0, ym, YM, 0)):
        if t != side:
            continue
        steps = [VEL[i][0] for i in group] + [0]
        for k, v in enumerate(raw(group)):
            to = x + steps[k]
            if fixed and not 0 <= to <= last_x:
                continue
            ref[k, pl.ds(to, 1), :] = v[row:row + 1]


def even(axis):
    return lax.axis_index(axis) % 2 == 0


def by_edge(axis, up, down):
    first = even(axis)
    return jnp.where(first, up, down), jnp.where(first, down, up)


def inner_columns(nx, body):
    def step(x, carry):
        body(x)
        return carry

    lax.fori_loop(1, nx - 1, step, 0)


def order_faces(xp, xm, x0, x1):
    for k in range(x0.shape[0]):
        x0[k], x1[k] = by_edge("gx", xp[k], xm[k])


def begin(x, t, f, solid, post, faces):
    nx, tiles = post.shape[1], post.shape[2] // 8
    rows = pl.ds(8 * t, 8)
    new = collide(f)
    flag = solid[x, rows, :].astype(jnp.float32)
    blocked = flag > 0.5
    for i in range(NQ):
        post[i, x, rows, :] = jnp.where(blocked, f[i] * MARK, new[i])

    def raw(group):
        return [new[i] for i in group] + [flag]

    send_faces(x, t, nx - 1, tiles - 1, raw, *faces)


def first_edge_kernel(f_hbm, solid_hbm, post, x0, x1, yp, ym, xp, xm, solid, sem):
    nx, ny = post.shape[1], post.shape[2]
    copies = []
    for n, x in enumerate((0, nx - 1)):
        at = pl.ds(x, 1)
        copies.append(pltpu.make_async_copy(solid_hbm.at[at], solid.at[at], sem.at[n]))
        copies.append(pltpu.make_async_copy(f_hbm.at[:, at], post.at[:, at], sem.at[2 + n]))
    for copy in copies:
        copy.start()
    for n, x in enumerate((0, nx - 1)):
        copies[2 * n].wait()
        copies[2 * n + 1].wait()
        for t in range(ny // 8):
            f = [post[i, x, pl.ds(8 * t, 8), :] for i in range(NQ)]
            begin(x, t, f, solid, post, (xp, xm, yp, ym))
    order_faces(xp, xm, x0, x1)


def first_inner_kernel(f_ref, solid, post_in, yp_in, ym_in, post, yp, ym):
    nx, ny = post.shape[1], post.shape[2]

    def body(x):
        for t in range(ny // 8):
            f = [f_ref[i, x, pl.ds(8 * t, 8), :] for i in range(NQ)]
            begin(x, t, f, solid, post, (None, None, yp, ym))

    inner_columns(nx, body)


def corner_kernel(yp, ym, r0, r1, y0, y1):
    planes, nx, _ = yp.shape
    ny = r0.shape[1]
    row = lax.broadcasted_iota(jnp.int32, yp.shape[1:], 0)

    def filled(ref, k, group, end):
        step, _, cz = VEL[group[k]]
        if step == 0 or cz:
            return ref[k]
        at = (XP if step == 1 else XM).index(group[k])
        right, left = by_edge("gx", r0[at, end:end + 1], r1[at, end:end + 1])
        return jnp.where(row == (0 if step == 1 else nx - 1), left if step == 1 else right, ref[k])

    for k in range(5):
        y0[pl.ds(k * nx, nx)], y1[pl.ds(k * nx, nx)] = by_edge(
            "gy", filled(yp, k, YP, ny - 1), filled(ym, k, YM, 0)
        )
    if planes > 5:
        y0[pl.ds(5 * nx, nx)], y1[pl.ds(5 * nx, nx)] = by_edge("gy", yp[5], ym[5])
        up = by_edge("gx", r0[5, ny - 1:ny], r1[5, ny - 1:ny])
        down = by_edge("gx", r0[5, 0:1], r1[5, 0:1])
        for n in range(2):
            at = pl.ds(6 * nx + n, 1)
            y0[at], y1[at] = by_edge("gy", up[1 - n], down[1 - n])
        rest = pl.ds(6 * nx + 2, 6)
        y0[rest] = y1[rest] = jnp.zeros((6, 128), jnp.float32)


def mark_x(r0, r1, flag_x0, flag_x1, hx):
    flags = by_edge("gx", flag_x0[5], flag_x1[5])
    for k in range(5):
        values = by_edge("gx", r0[k], r1[k])
        for side in range(2):
            hx[side, k] = jnp.where(flags[1 - side] > 0.5, MARK, values[1 - side])


def mark_y(s0, s1, flag_y0, flag_y1, hy):
    nx = hy.shape[2]
    row = lax.broadcasted_iota(jnp.int32, hy.shape[2:], 0)
    own = by_edge("gy", flag_y0[pl.ds(5 * nx, nx)], flag_y1[pl.ds(5 * nx, nx)])
    left, right = [
        by_edge("gy", flag_y0[pl.ds(6 * nx + n, 1)], flag_y1[pl.ds(6 * nx + n, 1)]) for n in range(2)
    ]
    for side, group in enumerate((YP, YM)):
        flags = {
            0: own[1 - side],
            1: jnp.where(row == 0, left[1 - side], pltpu.roll(own[1 - side], 1, 0)),
            -1: jnp.where(row == nx - 1, right[1 - side], pltpu.roll(own[1 - side], nx - 1, 0)),
        }
        for k in range(5):
            at = pl.ds(k * nx, nx)
            value = by_edge("gy", s0[at], s1[at])[1 - side]
            hy[side, k] = jnp.where(flags[VEL[group[k]][0]] > 0.5, MARK, value)


def arriving(post, hx, hy, x, t, i):
    nx, tiles = post.shape[1], post.shape[2] // 8
    cx, cy, cz = VEL[i]
    if isinstance(x, int) and not 0 <= x - cx < nx:
        view = hx.at[0, XP.index(i)] if cx == 1 else hx.at[1, XM.index(i)]
    else:
        view = post.at[i, x - cx]
    row = lax.broadcasted_iota(jnp.int32, (8, 128), 0)
    if cy == 1 and t == 0:
        v = pltpu.roll(view[pl.ds(0, 8), :], 1, 0)
        if hy is not None:
            v = jnp.where(row == 0, jnp.broadcast_to(hy[0, YP.index(i), pl.ds(x, 1), :], (8, 128)), v)
    elif cy == -1 and t == tiles - 1:
        v = pltpu.roll(view[pl.ds(8 * t, 8), :], 7, 0)
        if hy is not None:
            v = jnp.where(row == 7, jnp.broadcast_to(hy[1, YM.index(i), pl.ds(x, 1), :], (8, 128)), v)
    else:
        v = view[pl.ds(8 * t - cy, 8), :]
    return pltpu.roll(v, cz % 128, 1) if cz else v


def stream(post, hx, hy, x, t):
    own = [post[i, x, pl.ds(8 * t, 8), :] for i in range(NQ)]
    f = [own[0]]
    for i in range(1, NQ):
        v = arriving(post, hx, hy, x, t, i)
        f.append(jnp.where(v < EDGE, own[opposite(i)], v))
    return f, own, own[0] > EDGE


def advance(post, hx, hy, x, t, out, faces):
    nx, tiles = post.shape[1], post.shape[2] // 8
    f, own, fluid = stream(post, hx, hy, x, t)
    new = collide(f)
    for i in range(NQ):
        out[i, x, pl.ds(8 * t, 8), :] = jnp.where(fluid, new[i], own[i])
    send_faces(x, t, nx - 1, tiles - 1, lambda group: [new[i] for i in group], *faces)


def centre_kernel(post, r0, r1, flag_x0, flag_x1, out, xp, xm, hx):
    nx, ny = post.shape[1], post.shape[2]
    mark_x(r0, r1, flag_x0, flag_x1, hx)

    def body(x):
        for t in range(1, ny // 8 - 1):
            advance(post, hx, None, x, t, out, (xp, xm, None, None))

    body(0)
    body(nx - 1)
    inner_columns(nx, body)


def edge_kernel(post, hx, xp_in, xm_in, s0, s1, flag_y0, flag_y1, out_in, out, x0, x1, yp, ym, hy, xp, xm):
    nx, ny = post.shape[1], post.shape[2]
    mark_y(s0, s1, flag_y0, flag_y1, hy)
    for x in (0, nx - 1):
        for t in (0, ny // 8 - 1):
            advance(post, hx, hy, x, t, out, (xp, xm, yp, ym))
    for rows, up, down in (
        (pl.ds(0, 8), xp, xm),
        (pl.ds(8, ny - 16), xp_in, xm_in),
        (pl.ds(ny - 8, 8), xp, xm),
    ):
        for k in range(5):
            x0[k, rows, :], x1[k, rows, :] = by_edge("gx", up[k, rows, :], down[k, rows, :])


def rim_kernel(post, hy, out_in, yp_in, ym_in, out, yp, ym):
    def body(x):
        for t in (0, post.shape[2] // 8 - 1):
            advance(post, None, hy, x, t, out, (None, None, yp, ym))

    inner_columns(post.shape[1], body)


def last_centre_kernel(post, r0, r1, flag_x0, flag_x1, out_hbm, hx, stage, sem):
    nx, ny = post.shape[1], post.shape[2]
    mark_x(r0, r1, flag_x0, flag_x1, hx)

    def body(x):
        for t in range(ny // 8):
            f, own, fluid = stream(post, hx, None, x, t)
            for i in range(NQ):
                stage[i, x, pl.ds(8 * t, 8), :] = jnp.where(fluid, f[i], own[i] * (1.0 / MARK))

    def step(x, carry):
        body(x)
        return carry

    parts = sem.shape[0]
    size = nx // parts
    copies = []
    for p in range(parts):
        low, high = p * size, (p + 1) * size
        if p == 0:
            body(0)
        lax.fori_loop(max(low, 1), min(high, nx - 1), step, 0)
        if p == parts - 1:
            body(nx - 1)
        at = pl.ds(low, size)
        copies.append(pltpu.make_async_copy(stage.at[:, at], out_hbm.at[:, at], sem.at[p]))
        copies[-1].start()
    for copy in copies:
        copy.wait()


def last_kernel(post, hx, s0, s1, flag_y0, flag_y1, out_in, out_hbm, stage, hy, sem):
    nx, ny = post.shape[1], post.shape[2]
    mark_y(s0, s1, flag_y0, flag_y1, hy)
    copies = []
    for side, (t, group) in enumerate(((0, YP), (ny // 8 - 1, YM))):
        rows = pl.ds(8 * t, 8)
        fluid = [post[0, x, rows, :] > EDGE for x in range(nx)]
        for k, i in enumerate(group):
            for x in range(nx):
                v = arriving(post, hx, hy, x, t, i)
                v = jnp.where(v < EDGE, post[opposite(i), x, rows, :], v)
                stage[side, k, x] = jnp.where(fluid[x], v, post[i, x, rows, :] * (1.0 / MARK))
            copies.append(pltpu.make_async_copy(stage.at[side, k], out_hbm.at[i, :, rows], sem.at[side, k]))
            copies[-1].start()
    for copy in copies:
        copy.wait()


def swap(value, axis, edge):
    count = lax.axis_size(axis)
    pairs = [((2 * j + edge) % count, (2 * j + edge + 1) % count) for j in range(count // 2)]
    return lax.ppermute(value, axis, pairs + [(b, a) for a, b in pairs])


def local(populations, solid):
    _, nx, ny, nz = populations.shape
    f32 = jnp.float32
    anywhere = pl.BlockSpec(memory_space=pl.ANY)
    onchip = pl.BlockSpec(memory_space=pltpu.VMEM)
    state = pltpu.VMEM(populations.shape, f32)
    params = pltpu.CompilerParams(vmem_limit_bytes=24 << 20)

    def kernel(body, out_shape, in_specs, out_specs=None, scratch=(), aliases={}):
        return pl.pallas_call(
            body,
            out_shape=out_shape,
            in_specs=in_specs,
            out_specs=out_specs or (onchip,) * len(out_shape),
            scratch_shapes=list(scratch),
            input_output_aliases=aliases,
            compiler_params=params,
            cost_estimate=pl.CostEstimate(flops=1 << 24, bytes_accessed=1 << 22, transcendentals=0),
        )

    def held(value):
        return pltpu.with_memory_space_constraint(value, pltpu.VMEM)

    def face_x(planes):
        return jax.ShapeDtypeStruct((planes, ny, nz), f32)

    def face_y(planes):
        return jax.ShapeDtypeStruct((planes, nx, nz), f32)

    def swap_x(x0, x1):
        return swap(x0, "gx", 0), swap(x1, "gx", 1)

    def swap_y(yp, ym, r0, r1):
        rows = 5 * nx if yp.shape[0] == 5 else 6 * nx + 8
        shape = jax.ShapeDtypeStruct((rows, nz), f32)
        y0, y1 = kernel(corner_kernel, (shape,) * 2, [onchip] * 4)(yp, ym, r0, r1)
        return swap(y0, "gy", 0), swap(y1, "gy", 1)

    post, x0, x1, yp, ym = kernel(
        first_edge_kernel,
        (state, face_x(6), face_x(6), face_y(6), face_y(6)),
        [anywhere] * 2,
        scratch=[pltpu.VMEM((6, ny, nz), f32)] * 2
        + [pltpu.VMEM(solid.shape, jnp.int32), pltpu.SemaphoreType.DMA((4,))],
    )(
        pltpu.with_memory_space_constraint(populations, pltpu.HBM),
        pltpu.with_memory_space_constraint(solid, pltpu.HBM),
    )
    r0, r1 = swap_x(x0, x1)
    post, yp, ym = kernel(
        first_inner_kernel, (state, face_y(6), face_y(6)), [onchip] * 5, aliases={2: 0, 3: 1, 4: 2}
    )(held(populations), held(solid), held(post), yp, ym)
    flag_x = (r0, r1)
    s0, s1 = flag_y = swap_y(yp, ym, r0, r1)
    marked_x = jax.ShapeDtypeStruct((2, 5, ny, nz), f32)
    marked_y = jax.ShapeDtypeStruct((2, 5, nx, nz), f32)
    for _ in range(1, ITERS):
        post = held(post)
        new, xp, xm, hx = kernel(
            centre_kernel, (state, face_x(5), face_x(5), marked_x), [onchip] * 5
        )(post, r0, r1, *flag_x)
        new, x0, x1, yp, ym, hy = kernel(
            edge_kernel,
            (state, face_x(5), face_x(5), face_y(5), face_y(5), marked_y),
            [onchip] * 9,
            scratch=[pltpu.VMEM((5, ny, nz), f32)] * 2,
            aliases={8: 0},
        )(post, hx, xp, xm, s0, s1, *flag_y, held(new))
        r0, r1 = swap_x(x0, x1)
        new, yp, ym = kernel(
            rim_kernel, (state, face_y(5), face_y(5)), [onchip] * 5, aliases={2: 0, 3: 1, 4: 2}
        )(post, hy, held(new), yp, ym)
        s0, s1 = swap_y(yp, ym, r0, r1)
        post = new
    post = held(post)
    whole = jax.ShapeDtypeStruct(populations.shape, f32)
    out, hx = kernel(
        last_centre_kernel,
        (whole, marked_x),
        [onchip] * 5,
        (anywhere, onchip),
        scratch=[pltpu.VMEM(populations.shape, f32), pltpu.SemaphoreType.DMA((4,))],
    )(post, r0, r1, *flag_x)
    (out,) = kernel(
        last_kernel,
        (whole,),
        [onchip] * 6 + [anywhere],
        (anywhere,),
        scratch=[
            pltpu.VMEM((2, 5, nx, 8, nz), f32),
            pltpu.VMEM((2, 5, nx, nz), f32),
            pltpu.SemaphoreType.DMA((2, 5)),
        ],
        aliases={6: 0},
    )(post, hx, s0, s1, *flag_y, out)
    return out


def solution(mesh):
    in_specs = (P(None, "gx", "gy", None), P("gx", "gy", None))
    out_specs = P(None, "gx", "gy", None)
    return jax.shard_map(local, mesh=mesh, in_specs=in_specs, out_specs=out_specs, check_vma=False)
```

profile of v0, /device:TPU:0, one launch (start us, length us, event | category | flops | bytes accessed | tf_op | source)
XLA Modules:
  0.0 51.5 jit_solution(6910803771488604803)
XLA Ops:
  0.0 0.0 copy-start.1
  0.0 0.0 copy-start
  0.0 1.4 %shard_map.28 = (f32[19,16,32,128]{3,2,1,0:T(8,128)S(1)}, f32[6,32,128]{2,1,0:T(8,128)S(1)}, f32[6,32,128]{2,1,0:T(8,128)S(1)}, f32[6,16,128]{2,1,0:T(8,128)S(1)}, f32[6,16,128]{2,1,0:T(8,128)S(1)}) custom-call(f32[19,16,32,128]{3,2,1,0:T(8,128)} %f_ref.1, s32[16,32,128]{2,1,0:T(8,128)} %solid.1), custom_call_target="tpu_custom_call" | custom-call | flops 16777216 | bytes 4194304 | tf_op jit(solution)/shard_map/pallas_call | solution.py:381
  1.5 0.1 collective-permute-start
  1.6 4.6 %collective-permute-start.1 = (f32[6,32,128]{2,1,0:T(8,128)S(1)}, f32[6,32,128]{2,1,0:T(8,128)S(1)}, u32[]{:S(2)}, u32[]{:S(2)}) collective-permute-start(f32[6,32,128]{2,1,0:T(8,128)S(1)} %get-tuple-element.52), channel_id=1, source_target_pairs={{8,16},{24,32},{40,48},{56,64},{72,80},{88,96},{104,112},{120,0},{... | collective-permute-start | bytes 294920 | tf_op jit(solution)/shard_map/ppermute | solution.py:340
  6.1 0.0 copy-done.1
  6.1 0.0 copy-done
  6.1 1.8 %shard_map.29 = (f32[19,16,32,128]{3,2,1,0:T(8,128)S(1)}, f32[6,16,128]{2,1,0:T(8,128)S(1)}, f32[6,16,128]{2,1,0:T(8,128)S(1)}) custom-call(f32[19,16,32,128]{3,2,1,0:T(8,128)S(1)} %copy-done, s32[16,32,128]{2,1,0:T(8,128)S(1)} %copy-done.1, ...), custom_call_target="tpu_custom_call", output_to_operand_aliasing={{0}: (2, {}), {1}: (3, {}), {2}: (4, {})} | custom-call | flops 16777216 | bytes 4194304 | tf_op jit(solution)/shard_map/pallas_call | solution.py:392
  8.0 0.0 collective-permute-done.r0.flag_x0
  8.0 0.5 collective-permute-done.1.r1.flag_x1
  8.5 3.7 %collective-permute-start.2 = (f32[104,128]{1,0:T(8,128)S(1)}, f32[104,128]{1,0:T(8,128)S(1)}, u32[]{:S(2)}, u32[]{:S(2)}) collective-permute-start(f32[104,128]{1,0:T(8,128)S(1)} %get-tuple-element.58), channel_id=1, source_target_pairs={{0,1},{2,3},{4,5},{6,7},{1,0},{3,2},{5,4},{7,6},{8,9},{10,11},{12,... | collective-permute-start | bytes 159752 | tf_op jit(solution)/shard_map/ppermute | solution.py:340
  12.1 2.3 %collective-permute-start.3 = (f32[104,128]{1,0:T(8,128)S(1)}, f32[104,128]{1,0:T(8,128)S(1)}, u32[]{:S(2)}, u32[]{:S(2)}) collective-permute-start(f32[104,128]{1,0:T(8,128)S(1)} %get-tuple-element.59), channel_id=1, source_target_pairs={{1,2},{3,4},{5,6},{7,0},{2,1},{4,3},{6,5},{0,7},{9,10},{11,12},{13... | collective-permute-start | bytes 159752 | tf_op jit(solution)/shard_map/ppermute | solution.py:340
  14.4 2.2 %shard_map.30 = (f32[19,16,32,128]{3,2,1,0:T(8,128)S(1)}, f32[5,32,128]{2,1,0:T(8,128)S(1)}, f32[5,32,128]{2,1,0:T(8,128)S(1)}, f32[2,5,32,128]{3,2,1,0:T(8,128)S(1)}) custom-call(f32[19,16,32,128]{3,2,1,0:T(8,128)S(1)} %get-tuple-element.50.post, f32[6,32,128]{2,1,0:T(8,128)S(1)} %collective-permute-done.r0.flag_x0, ...), custom_call_target="tpu_custom_call" | custom-call | flops 16777216 | bytes 4194304 | tf_op jit(solution)/shard_map/pallas_call | solution.py:401
  16.6 0.0 collective-permute-done.2.s0.flag_y0
  16.6 3.3 %collective-permute-done.3.s1.flag_y1 = f32[104,128]{1,0:T(8,128)S(1)} collective-permute-done((f32[104,128]{1,0:T(8,128)S(1)}, f32[104,128]{1,0:T(8,128)S(1)}, u32[]{:S(2)}, u32[]{:S(2)}) %collective-permute-start.3) | collective-permute-done | bytes 53280 | tf_op jit(solution)/shard_map/ppermute | solution.py:340
  19.9 0.2 shard_map.32
  20.1 0.1 collective-permute-start.4
  20.2 1.9 %collective-permute-start.5 = (f32[5,32,128]{2,1,0:T(8,128)S(1)}, f32[5,32,128]{2,1,0:T(8,128)S(1)}, u32[]{:S(2)}, u32[]{:S(2)}) collective-permute-start(f32[5,32,128]{2,1,0:T(8,128)S(1)} %get-tuple-element.67), channel_id=1, source_target_pairs={{8,16},{24,32},{40,48},{56,64},{72,80},{88,96},{104,112},{120,0},{... | collective-permute-start | bytes 245768 | tf_op jit(solution)/shard_map/ppermute | solution.py:340
  22.1 2.0 %shard_map.33 = (f32[19,16,32,128]{3,2,1,0:T(8,128)S(1)}, f32[5,16,128]{2,1,0:T(8,128)S(1)}, f32[5,16,128]{2,1,0:T(8,128)S(1)}) custom-call(f32[19,16,32,128]{3,2,1,0:T(8,128)S(1)} %get-tuple-element.50.post, f32[2,5,16,128]{3,2,1,0:T(8,128)S(1)} %get-tuple-element.61.hy, ...), custom_call_target="tpu_custom_call", output_to_operand_aliasing={{0}: (2, {}), {1}: (3, {}), {2}: (4, {})} | custom-call | flops 16777216 | bytes 4194304 | tf_op jit(solution)/shard_map/pallas_call | solution.py:412
  24.1 0.0 collective-permute-done.4.r0
  24.1 2.2 %collective-permute-done.5.r1 = f32[5,32,128]{2,1,0:T(8,128)S(1)} collective-permute-done((f32[5,32,128]{2,1,0:T(8,128)S(1)}, f32[5,32,128]{2,1,0:T(8,128)S(1)}, u32[]{:S(2)}, u32[]{:S(2)}) %collective-permute-start.5) | collective-permute-done | bytes 81952 | tf_op jit(solution)/shard_map/ppermute | solution.py:340
  26.3 0.1 collective-permute-start.6
  26.4 4.4 %collective-permute-start.7 = (f32[80,128]{1,0:T(8,128)S(1)}, f32[80,128]{1,0:T(8,128)S(1)}, u32[]{:S(2)}, u32[]{:S(2)}) collective-permute-start(f32[80,128]{1,0:T(8,128)S(1)} %get-tuple-element.74), channel_id=1, source_target_pairs={{1,2},{3,4},{5,6},{7,0},{2,1},{4,3},{6,5},{0,7},{9,10},{11,12},{13... | collective-permute-start | bytes 122888 | tf_op jit(solution)/shard_map/ppermute | solution.py:340
  30.9 2.2 %shard_map.34 = (f32[19,16,32,128]{3,2,1,0:T(8,128)S(1)}, f32[5,32,128]{2,1,0:T(8,128)S(1)}, f32[5,32,128]{2,1,0:T(8,128)S(1)}, f32[2,5,32,128]{3,2,1,0:T(8,128)S(1)}) custom-call(f32[19,16,32,128]{3,2,1,0:T(8,128)S(1)} %get-tuple-element.65.post, f32[5,32,128]{2,1,0:T(8,128)S(1)} %collective-permute-done.4.r0, f32[5,32,128]{2,1,0:T(8,128)S(1)} %collective-permute-done.5.r1, ...), custom_call_target="tpu_custom_call" | custom-call | flops 16777216 | bytes 4194304 | tf_op jit(solution)/shard_map/pallas_call | solution.py:401
  33.1 0.0 collective-permute-done.6.s0
  33.1 1.0 %collective-permute-done.7.s1 = f32[80,128]{1,0:T(8,128)S(1)} collective-permute-done((f32[80,128]{1,0:T(8,128)S(1)}, f32[80,128]{1,0:T(8,128)S(1)}, u32[]{:S(2)}, u32[]{:S(2)}) %collective-permute-start.7) | collective-permute-done | bytes 40992 | tf_op jit(solution)/shard_map/ppermute | solution.py:340
  34.1 0.2 shard_map.36
  34.3 0.1 collective-permute-start.8
  34.4 0.7 %collective-permute-start.9 = (f32[5,32,128]{2,1,0:T(8,128)S(1)}, f32[5,32,128]{2,1,0:T(8,128)S(1)}, u32[]{:S(2)}, u32[]{:S(2)}) collective-permute-start(f32[5,32,128]{2,1,0:T(8,128)S(1)} %get-tuple-element.82), channel_id=1, source_target_pairs={{8,16},{24,32},{40,48},{56,64},{72,80},{88,96},{104,112},{120,0},{... | collective-permute-start | bytes 245768 | tf_op jit(solution)/shard_map/ppermute | solution.py:340
  35.1 2.0 %shard_map.37 = (f32[19,16,32,128]{3,2,1,0:T(8,128)S(1)}, f32[5,16,128]{2,1,0:T(8,128)S(1)}, f32[5,16,128]{2,1,0:T(8,128)S(1)}) custom-call(f32[19,16,32,128]{3,2,1,0:T(8,128)S(1)} %get-tuple-element.65.post, f32[2,5,16,128]{3,2,1,0:T(8,128)S(1)} %get-tuple-element.76.hy, ...), custom_call_target="tpu_custom_call", output_to_operand_aliasing={{0}: (2, {}), {1}: (3, {}), {2}: (4, {})} | custom-call | flops 16777216 | bytes 4194304 | tf_op jit(solution)/shard_map/pallas_call | solution.py:412
  37.1 0.0 collective-permute-done.8.r0
  37.1 3.4 %collective-permute-done.9.r1 = f32[5,32,128]{2,1,0:T(8,128)S(1)} collective-permute-done((f32[5,32,128]{2,1,0:T(8,128)S(1)}, f32[5,32,128]{2,1,0:T(8,128)S(1)}, u32[]{:S(2)}, u32[]{:S(2)}) %collective-permute-start.9) | collective-permute-done | bytes 81952 | tf_op jit(solution)/shard_map/ppermute | solution.py:340
  40.5 2.3 %collective-permute-start.10 = (f32[80,128]{1,0:T(8,128)S(1)}, f32[80,128]{1,0:T(8,128)S(1)}, u32[]{:S(2)}, u32[]{:S(2)}) collective-permute-start(f32[80,128]{1,0:T(8,128)S(1)} %get-tuple-element.86), channel_id=1, source_target_pairs={{0,1},{2,3},{4,5},{6,7},{1,0},{3,2},{5,4},{7,6},{8,9},{10,11},{12,... | collective-permute-start | bytes 122888 | tf_op jit(solution)/shard_map/ppermute | solution.py:340
  42.8 2.2 %collective-permute-start.11 = (f32[80,128]{1,0:T(8,128)S(1)}, f32[80,128]{1,0:T(8,128)S(1)}, u32[]{:S(2)}, u32[]{:S(2)}) collective-permute-start(f32[80,128]{1,0:T(8,128)S(1)} %get-tuple-element.87), channel_id=1, source_target_pairs={{1,2},{3,4},{5,6},{7,0},{2,1},{4,3},{6,5},{0,7},{9,10},{11,12},{13... | collective-permute-start | bytes 122888 | tf_op jit(solution)/shard_map/ppermute | solution.py:340
  45.1 2.9 %shard_map.38 = (f32[19,16,32,128]{3,2,1,0:T(8,128)}, f32[2,5,32,128]{3,2,1,0:T(8,128)S(1)}) custom-call(f32[19,16,32,128]{3,2,1,0:T(8,128)S(1)} %get-tuple-element.80.post, f32[5,32,128]{2,1,0:T(8,128)S(1)} %collective-permute-done.8.r0, f32[5,32,128]{2,1,0:T(8,128)S(1)} %collective-permute-done.9.r1, f32[6,32,128]{2,1,0:T(8,128)S(1)} %collective-permute-done.r0.flag_x0, ...), custom_call_target="tpu_custom_call" | custom-call | flops 16777216 | bytes 4194304 | tf_op jit(solution)/shard_map/pallas_call | solution.py:419
  47.9 0.0 collective-permute-done.10.s0
  47.9 2.5 %collective-permute-done.11.s1 = f32[80,128]{1,0:T(8,128)S(1)} collective-permute-done((f32[80,128]{1,0:T(8,128)S(1)}, f32[80,128]{1,0:T(8,128)S(1)}, u32[]{:S(2)}, u32[]{:S(2)}) %collective-permute-start.11) | collective-permute-done | bytes 40992 | tf_op jit(solution)/shard_map/ppermute | solution.py:340
  50.4 1.1 %shard_map.40 = f32[19,16,32,128]{3,2,1,0:T(8,128)} custom-call(f32[19,16,32,128]{3,2,1,0:T(8,128)S(1)} %get-tuple-element.80.post, f32[2,5,32,128]{3,2,1,0:T(8,128)S(1)} %get-tuple-element.83.hx, f32[80,128]{1,0:T(8,128)S(1)} %collective-permute-done.10.s0, f32[80,128]{1,0:T(8,128)S(1)} %collective-permute-done.11.s1, ...), custom_call_target="tpu_custom_call", output_to_operand_aliasing={{}: (6, {})} | custom-call | flops 16777216 | bytes 4194304 | tf_op jit(solution)/shard_map/pallas_call | solution.py:426
  (3 shorter events, 0.1 us)
Async XLA Ops:
  0.0 6.1 %copy-start.1 = (s32[16,32,128]{2,1,0:T(8,128)S(1)}, s32[16,32,128]{2,1,0:T(8,128)}, u32[]{:S(2)}) copy-start(s32[16,32,128]{2,1,0:T(8,128)} %solid.1) | copy-start | bytes 786436
  0.0 6.1 %copy-start = (f32[19,16,32,128]{3,2,1,0:T(8,128)S(1)}, f32[19,16,32,128]{3,2,1,0:T(8,128)}, u32[]{:S(2)}) copy-start(f32[19,16,32,128]{3,2,1,0:T(8,128)} %f_ref.1) | copy-start | bytes 14942212
  1.5 6.5 %collective-permute-start = (f32[6,32,128]{2,1,0:T(8,128)S(1)}, f32[6,32,128]{2,1,0:T(8,128)S(1)}, u32[]{:S(2)}, u32[]{:S(2)}) collective-permute-start(f32[6,32,128]{2,1,0:T(8,128)S(1)} %get-tuple-element.51), channel_id=1, source_target_pairs={{0,8},{16,24},{32,40},{48,56},{64,72},{80,88},{96,104},{112,120},{... | collective-permute-start | bytes 294920 | tf_op jit(solution)/shard_map/ppermute | solution.py:340
  1.6 6.9 %collective-permute-start.1 = (f32[6,32,128]{2,1,0:T(8,128)S(1)}, f32[6,32,128]{2,1,0:T(8,128)S(1)}, u32[]{:S(2)}, u32[]{:S(2)}) collective-permute-start(f32[6,32,128]{2,1,0:T(8,128)S(1)} %get-tuple-element.52), channel_id=1, source_target_pairs={{8,16},{24,32},{40,48},{56,64},{72,80},{88,96},{104,112},{120,0},{... | collective-permute-start | bytes 294920 | tf_op jit(solution)/shard_map/ppermute | solution.py:340
  8.5 8.1 %collective-permute-start.2 = (f32[104,128]{1,0:T(8,128)S(1)}, f32[104,128]{1,0:T(8,128)S(1)}, u32[]{:S(2)}, u32[]{:S(2)}) collective-permute-start(f32[104,128]{1,0:T(8,128)S(1)} %get-tuple-element.58), channel_id=1, source_target_pairs={{0,1},{2,3},{4,5},{6,7},{1,0},{3,2},{5,4},{7,6},{8,9},{10,11},{12,... | collective-permute-start | bytes 159752 | tf_op jit(solution)/shard_map/ppermute | solution.py:340
  12.1 7.7 %collective-permute-start.3 = (f32[104,128]{1,0:T(8,128)S(1)}, f32[104,128]{1,0:T(8,128)S(1)}, u32[]{:S(2)}, u32[]{:S(2)}) collective-permute-start(f32[104,128]{1,0:T(8,128)S(1)} %get-tuple-element.59), channel_id=1, source_target_pairs={{1,2},{3,4},{5,6},{7,0},{2,1},{4,3},{6,5},{0,7},{9,10},{11,12},{13... | collective-permute-start | bytes 159752 | tf_op jit(solution)/shard_map/ppermute | solution.py:340
  20.1 4.0 %collective-permute-start.4 = (f32[5,32,128]{2,1,0:T(8,128)S(1)}, f32[5,32,128]{2,1,0:T(8,128)S(1)}, u32[]{:S(2)}, u32[]{:S(2)}) collective-permute-start(f32[5,32,128]{2,1,0:T(8,128)S(1)} %get-tuple-element.66), channel_id=1, source_target_pairs={{0,8},{16,24},{32,40},{48,56},{64,72},{80,88},{96,104},{112,120},{... | collective-permute-start | bytes 245768 | tf_op jit(solution)/shard_map/ppermute | solution.py:340
  20.2 6.1 %collective-permute-start.5 = (f32[5,32,128]{2,1,0:T(8,128)S(1)}, f32[5,32,128]{2,1,0:T(8,128)S(1)}, u32[]{:S(2)}, u32[]{:S(2)}) collective-permute-start(f32[5,32,128]{2,1,0:T(8,128)S(1)} %get-tuple-element.67), channel_id=1, source_target_pairs={{8,16},{24,32},{40,48},{56,64},{72,80},{88,96},{104,112},{120,0},{... | collective-permute-start | bytes 245768 | tf_op jit(solution)/shard_map/ppermute | solution.py:340
  26.3 6.7 %collective-permute-start.6 = (f32[80,128]{1,0:T(8,128)S(1)}, f32[80,128]{1,0:T(8,128)S(1)}, u32[]{:S(2)}, u32[]{:S(2)}) collective-permute-start(f32[80,128]{1,0:T(8,128)S(1)} %get-tuple-element.73), channel_id=1, source_target_pairs={{0,1},{2,3},{4,5},{6,7},{1,0},{3,2},{5,4},{7,6},{8,9},{10,11},{12,... | collective-permute-start | bytes 122888 | tf_op jit(solution)/shard_map/ppermute | solution.py:340
  26.4 7.7 %collective-permute-start.7 = (f32[80,128]{1,0:T(8,128)S(1)}, f32[80,128]{1,0:T(8,128)S(1)}, u32[]{:S(2)}, u32[]{:S(2)}) collective-permute-start(f32[80,128]{1,0:T(8,128)S(1)} %get-tuple-element.74), channel_id=1, source_target_pairs={{1,2},{3,4},{5,6},{7,0},{2,1},{4,3},{6,5},{0,7},{9,10},{11,12},{13... | collective-permute-start | bytes 122888 | tf_op jit(solution)/shard_map/ppermute | solution.py:340
  34.3 2.8 %collective-permute-start.8 = (f32[5,32,128]{2,1,0:T(8,128)S(1)}, f32[5,32,128]{2,1,0:T(8,128)S(1)}, u32[]{:S(2)}, u32[]{:S(2)}) collective-permute-start(f32[5,32,128]{2,1,0:T(8,128)S(1)} %get-tuple-element.81), channel_id=1, source_target_pairs={{0,8},{16,24},{32,40},{48,56},{64,72},{80,88},{96,104},{112,120},{... | collective-permute-start | bytes 245768 | tf_op jit(solution)/shard_map/ppermute | solution.py:340
  34.4 6.1 %collective-permute-start.9 = (f32[5,32,128]{2,1,0:T(8,128)S(1)}, f32[5,32,128]{2,1,0:T(8,128)S(1)}, u32[]{:S(2)}, u32[]{:S(2)}) collective-permute-start(f32[5,32,128]{2,1,0:T(8,128)S(1)} %get-tuple-element.82), channel_id=1, source_target_pairs={{8,16},{24,32},{40,48},{56,64},{72,80},{88,96},{104,112},{120,0},{... | collective-permute-start | bytes 245768 | tf_op jit(solution)/shard_map/ppermute | solution.py:340
  40.5 7.4 %collective-permute-start.10 = (f32[80,128]{1,0:T(8,128)S(1)}, f32[80,128]{1,0:T(8,128)S(1)}, u32[]{:S(2)}, u32[]{:S(2)}) collective-permute-start(f32[80,128]{1,0:T(8,128)S(1)} %get-tuple-element.86), channel_id=1, source_target_pairs={{0,1},{2,3},{4,5},{6,7},{1,0},{3,2},{5,4},{7,6},{8,9},{10,11},{12,... | collective-permute-start | bytes 122888 | tf_op jit(solution)/shard_map/ppermute | solution.py:340
  42.8 7.6 %collective-permute-start.11 = (f32[80,128]{1,0:T(8,128)S(1)}, f32[80,128]{1,0:T(8,128)S(1)}, u32[]{:S(2)}, u32[]{:S(2)}) collective-permute-start(f32[80,128]{1,0:T(8,128)S(1)} %get-tuple-element.87), channel_id=1, source_target_pairs={{1,2},{3,4},{5,6},{7,0},{2,1},{4,3},{6,5},{0,7},{9,10},{11,12},{13... | collective-permute-start | bytes 122888 | tf_op jit(solution)/shard_map/ppermute | solution.py:340
where the time goes:
time: 51.6 us; the launch traced here: 51.5 us
  starting transfers between devices  22.4 us (43%)
  Pallas kernels  16 us (31%)
  waiting for transfers between devices  12.8 us (25%)
    ppermute x12, starting transfers between devices, swap(): return lax.ppermute(value, axis, pairs + [(b, a) for a, b in pairs])  22.4 us
    ppermute x12, waiting for transfers between devices, swap(): return lax.ppermute(value, axis, pairs + [(b, a) for a, b in pairs])  12.8 us
    pallas_call x2, Pallas kernels, local(): kernel(centre_kernel, (state, face_x(5), face_x(5), marked_x), [onchip] * 5)  4.38 us
    pallas_call x2, Pallas kernels, local(): kernel(rim_kernel, (state, face_y(5), face_y(5)), [onchip] * 5, aliases={...  3.98 us
    pallas_call x1, Pallas kernels, local(): kernel(last_centre_kernel, (whole, marked_x), [onchip] * 5, (anywhere, on...  2.86 us
    pallas_call x1, Pallas kernels, local(): kernel(first_inner_kernel, (state, face_y(6), face_y(6)), [onchip] * 5, a...  1.82 us
    pallas_call x1, Pallas kernels, local(): kernel(first_edge_kernel, (state, face_x(6), face_x(6), face_y(6), face_y...  1.44 us
    pallas_call x1, Pallas kernels, local(): kernel(last_kernel, (whole,), [onchip] * 6 + [anywhere], (anywhere,), scr...  1.06 us
  transfers between devices with their start and end apart: 12, of which 6 were waited for; matrix products, arithmetic and copies ran while one was open for 0% of the time, Pallas kernels for 25%

commit v1 on v0

--- a/solution.py
+++ b/solution.py
@@ -98,12 +98,12 @@
     return jnp.where(first, up, down), jnp.where(first, down, up)
 
 
-def inner_columns(nx, body):
+def inner_columns(nx, body, unroll=1):
     def step(x, carry):
         body(x)
         return carry
 
-    lax.fori_loop(1, nx - 1, step, 0)
+    lax.fori_loop(1, nx - 1, step, 0, unroll=unroll)
 
 
 def order_faces(xp, xm, x0, x1):
@@ -282,7 +282,7 @@
         for t in (0, post.shape[2] // 8 - 1):
             advance(post, None, hy, x, t, out, (None, None, yp, ym))
 
-    inner_columns(post.shape[1], body)
+    inner_columns(post.shape[1], body, 2)
 
 
 def last_centre_kernel(post, r0, r1, flag_x0, flag_x1, out_hbm, hx, stage, sem):

time: 51.6 us -> 51.6 us (level)
  Pallas kernels: 16 us -> 15.1 us
  waiting for transfers between devices: 12.8 us -> 13.7 us
    ppermute x12, waiting for transfers between devices: 12.8 us -> 13.7 us  [swap(): return lax.ppermute(value, axis, pairs + [(b, a) for a, b in pairs])]
    pallas_call x2, Pallas kernels: 3.98 us -> 3.07 us  [local(): kernel(rim_kernel, (state, face_y(5), face_y(5)), [onchip] * 5, aliases={...]
  transfers between devices with their start and end apart: 12 -> 12, of which waited for: 6 -> 6; matrix products, arithmetic and copies ran while one was open for 0% -> 0% of each run, Pallas kernels for 25% -> 24%
where the time goes in v1:
time: 51.6 us; the launch traced here: 51.5 us
  starting transfers between devices  22.4 us (43%)
  Pallas kernels  15.1 us (29%)
  waiting for transfers between devices  13.7 us (27%)
    ppermute x12, starting transfers between devices, swap(): return lax.ppermute(value, axis, pairs + [(b, a) for a, b in pairs])  22.4 us
    ppermute x12, waiting for transfers between devices, swap(): return lax.ppermute(value, axis, pairs + [(b, a) for a, b in pairs])  13.7 us
    pallas_call x2, Pallas kernels, local(): kernel(centre_kernel, (state, face_x(5), face_x(5), marked_x), [onchip] * 5)  4.38 us
    pallas_call x2, Pallas kernels, local(): kernel(rim_kernel, (state, face_y(5), face_y(5)), [onchip] * 5, aliases={...  3.07 us
    pallas_call x1, Pallas kernels, local(): kernel(last_centre_kernel, (whole, marked_x), [onchip] * 5, (anywhere, on...  2.86 us
    pallas_call x1, Pallas kernels, local(): kernel(first_inner_kernel, (state, face_y(6), face_y(6)), [onchip] * 5, a...  1.82 us
    pallas_call x1, Pallas kernels, local(): kernel(first_edge_kernel, (state, face_x(6), face_x(6), face_y(6), face_y...  1.44 us
    pallas_call x1, Pallas kernels, local(): kernel(last_kernel, (whole,), [onchip] * 6 + [anywhere], (anywhere,), scr...  1.06 us
  transfers between devices with their start and end apart: 12, of which 6 were waited for; matrix products, arithmetic and copies ran while one was open for 0% of the time, Pallas kernels for 24%

profile of v1, /device:TPU:0, one launch (start us, length us, event | category | flops | bytes accessed | tf_op | source)
XLA Modules:
  0.0 51.5 jit_solution(4613380020440173607)
XLA Ops:
  0.0 0.0 copy-start.1
  0.0 0.0 copy-start
  0.0 1.4 %shard_map.28 = (f32[19,16,32,128]{3,2,1,0:T(8,128)S(1)}, f32[6,32,128]{2,1,0:T(8,128)S(1)}, f32[6,32,128]{2,1,0:T(8,128)S(1)}, f32[6,16,128]{2,1,0:T(8,128)S(1)}, f32[6,16,128]{2,1,0:T(8,128)S(1)}) custom-call(f32[19,16,32,128]{3,2,1,0:T(8,128)} %f_ref.1, s32[16,32,128]{2,1,0:T(8,128)} %solid.1), custom_call_target="tpu_custom_call" | custom-call | flops 16777216 | bytes 4194304 | tf_op jit(solution)/shard_map/pallas_call | solution.py:381
  1.5 0.1 collective-permute-start
  1.6 4.6 %collective-permute-start.1 = (f32[6,32,128]{2,1,0:T(8,128)S(1)}, f32[6,32,128]{2,1,0:T(8,128)S(1)}, u32[]{:S(2)}, u32[]{:S(2)}) collective-permute-start(f32[6,32,128]{2,1,0:T(8,128)S(1)} %get-tuple-element.52), channel_id=1, source_target_pairs={{8,16},{24,32},{40,48},{56,64},{72,80},{88,96},{104,112},{120,0},{... | collective-permute-start | bytes 294920 | tf_op jit(solution)/shard_map/ppermute | solution.py:340
  6.1 0.0 copy-done.1
  6.1 0.0 copy-done
  6.1 1.8 %shard_map.29 = (f32[19,16,32,128]{3,2,1,0:T(8,128)S(1)}, f32[6,16,128]{2,1,0:T(8,128)S(1)}, f32[6,16,128]{2,1,0:T(8,128)S(1)}) custom-call(f32[19,16,32,128]{3,2,1,0:T(8,128)S(1)} %copy-done, s32[16,32,128]{2,1,0:T(8,128)S(1)} %copy-done.1, ...), custom_call_target="tpu_custom_call", output_to_operand_aliasing={{0}: (2, {}), {1}: (3, {}), {2}: (4, {})} | custom-call | flops 16777216 | bytes 4194304 | tf_op jit(solution)/shard_map/pallas_call | solution.py:392
  8.0 0.0 collective-permute-done.r0.flag_x0
  8.0 0.5 collective-permute-done.1.r1.flag_x1
  8.5 3.7 %collective-permute-start.2 = (f32[104,128]{1,0:T(8,128)S(1)}, f32[104,128]{1,0:T(8,128)S(1)}, u32[]{:S(2)}, u32[]{:S(2)}) collective-permute-start(f32[104,128]{1,0:T(8,128)S(1)} %get-tuple-element.58), channel_id=1, source_target_pairs={{0,1},{2,3},{4,5},{6,7},{1,0},{3,2},{5,4},{7,6},{8,9},{10,11},{12,... | collective-permute-start | bytes 159752 | tf_op jit(solution)/shard_map/ppermute | solution.py:340
  12.1 2.3 %collective-permute-start.3 = (f32[104,128]{1,0:T(8,128)S(1)}, f32[104,128]{1,0:T(8,128)S(1)}, u32[]{:S(2)}, u32[]{:S(2)}) collective-permute-start(f32[104,128]{1,0:T(8,128)S(1)} %get-tuple-element.59), channel_id=1, source_target_pairs={{1,2},{3,4},{5,6},{7,0},{2,1},{4,3},{6,5},{0,7},{9,10},{11,12},{13... | collective-permute-start | bytes 159752 | tf_op jit(solution)/shard_map/ppermute | solution.py:340
  14.4 2.2 %shard_map.30 = (f32[19,16,32,128]{3,2,1,0:T(8,128)S(1)}, f32[5,32,128]{2,1,0:T(8,128)S(1)}, f32[5,32,128]{2,1,0:T(8,128)S(1)}, f32[2,5,32,128]{3,2,1,0:T(8,128)S(1)}) custom-call(f32[19,16,32,128]{3,2,1,0:T(8,128)S(1)} %get-tuple-element.50.post, f32[6,32,128]{2,1,0:T(8,128)S(1)} %collective-permute-done.r0.flag_x0, ...), custom_call_target="tpu_custom_call" | custom-call | flops 16777216 | bytes 4194304 | tf_op jit(solution)/shard_map/pallas_call | solution.py:401
  16.6 0.0 collective-permute-done.2.s0.flag_y0
  16.6 3.3 %collective-permute-done.3.s1.flag_y1 = f32[104,128]{1,0:T(8,128)S(1)} collective-permute-done((f32[104,128]{1,0:T(8,128)S(1)}, f32[104,128]{1,0:T(8,128)S(1)}, u32[]{:S(2)}, u32[]{:S(2)}) %collective-permute-start.3) | collective-permute-done | bytes 53280 | tf_op jit(solution)/shard_map/ppermute | solution.py:340
  19.9 0.2 shard_map.32
  20.1 0.1 collective-permute-start.4
  20.2 1.9 %collective-permute-start.5 = (f32[5,32,128]{2,1,0:T(8,128)S(1)}, f32[5,32,128]{2,1,0:T(8,128)S(1)}, u32[]{:S(2)}, u32[]{:S(2)}) collective-permute-start(f32[5,32,128]{2,1,0:T(8,128)S(1)} %get-tuple-element.67), channel_id=1, source_target_pairs={{8,16},{24,32},{40,48},{56,64},{72,80},{88,96},{104,112},{120,0},{... | collective-permute-start | bytes 245768 | tf_op jit(solution)/shard_map/ppermute | solution.py:340
  22.1 1.5 %shard_map.33 = (f32[19,16,32,128]{3,2,1,0:T(8,128)S(1)}, f32[5,16,128]{2,1,0:T(8,128)S(1)}, f32[5,16,128]{2,1,0:T(8,128)S(1)}) custom-call(f32[19,16,32,128]{3,2,1,0:T(8,128)S(1)} %get-tuple-element.50.post, f32[2,5,16,128]{3,2,1,0:T(8,128)S(1)} %get-tuple-element.61.hy, ...), custom_call_target="tpu_custom_call", output_to_operand_aliasing={{0}: (2, {}), {1}: (3, {}), {2}: (4, {})} | custom-call | flops 16777216 | bytes 4194304 | tf_op jit(solution)/shard_map/pallas_call | solution.py:412
  23.6 0.0 collective-permute-done.4.r0
  23.6 2.7 %collective-permute-done.5.r1 = f32[5,32,128]{2,1,0:T(8,128)S(1)} collective-permute-done((f32[5,32,128]{2,1,0:T(8,128)S(1)}, f32[5,32,128]{2,1,0:T(8,128)S(1)}, u32[]{:S(2)}, u32[]{:S(2)}) %collective-permute-start.5) | collective-permute-done | bytes 81952 | tf_op jit(solution)/shard_map/ppermute | solution.py:340
  26.3 0.1 collective-permute-start.6
  26.4 4.4 %collective-permute-start.7 = (f32[80,128]{1,0:T(8,128)S(1)}, f32[80,128]{1,0:T(8,128)S(1)}, u32[]{:S(2)}, u32[]{:S(2)}) collective-permute-start(f32[80,128]{1,0:T(8,128)S(1)} %get-tuple-element.74), channel_id=1, source_target_pairs={{1,2},{3,4},{5,6},{7,0},{2,1},{4,3},{6,5},{0,7},{9,10},{11,12},{13... | collective-permute-start | bytes 122888 | tf_op jit(solution)/shard_map/ppermute | solution.py:340
  30.9 2.2 %shard_map.34 = (f32[19,16,32,128]{3,2,1,0:T(8,128)S(1)}, f32[5,32,128]{2,1,0:T(8,128)S(1)}, f32[5,32,128]{2,1,0:T(8,128)S(1)}, f32[2,5,32,128]{3,2,1,0:T(8,128)S(1)}) custom-call(f32[19,16,32,128]{3,2,1,0:T(8,128)S(1)} %get-tuple-element.65.post, f32[5,32,128]{2,1,0:T(8,128)S(1)} %collective-permute-done.4.r0, f32[5,32,128]{2,1,0:T(8,128)S(1)} %collective-permute-done.5.r1, ...), custom_call_target="tpu_custom_call" | custom-call | flops 16777216 | bytes 4194304 | tf_op jit(solution)/shard_map/pallas_call | solution.py:401
  33.1 0.0 collective-permute-done.6.s0
  33.1 1.0 %collective-permute-done.7.s1 = f32[80,128]{1,0:T(8,128)S(1)} collective-permute-done((f32[80,128]{1,0:T(8,128)S(1)}, f32[80,128]{1,0:T(8,128)S(1)}, u32[]{:S(2)}, u32[]{:S(2)}) %collective-permute-start.7) | collective-permute-done | bytes 40992 | tf_op jit(solution)/shard_map/ppermute | solution.py:340
  34.1 0.2 shard_map.36
  34.3 0.1 collective-permute-start.8
  34.4 0.7 %collective-permute-start.9 = (f32[5,32,128]{2,1,0:T(8,128)S(1)}, f32[5,32,128]{2,1,0:T(8,128)S(1)}, u32[]{:S(2)}, u32[]{:S(2)}) collective-permute-start(f32[5,32,128]{2,1,0:T(8,128)S(1)} %get-tuple-element.82), channel_id=1, source_target_pairs={{8,16},{24,32},{40,48},{56,64},{72,80},{88,96},{104,112},{120,0},{... | collective-permute-start | bytes 245768 | tf_op jit(solution)/shard_map/ppermute | solution.py:340
  35.1 1.5 %shard_map.37 = (f32[19,16,32,128]{3,2,1,0:T(8,128)S(1)}, f32[5,16,128]{2,1,0:T(8,128)S(1)}, f32[5,16,128]{2,1,0:T(8,128)S(1)}) custom-call(f32[19,16,32,128]{3,2,1,0:T(8,128)S(1)} %get-tuple-element.65.post, f32[2,5,16,128]{3,2,1,0:T(8,128)S(1)} %get-tuple-element.76.hy, ...), custom_call_target="tpu_custom_call", output_to_operand_aliasing={{0}: (2, {}), {1}: (3, {}), {2}: (4, {})} | custom-call | flops 16777216 | bytes 4194304 | tf_op jit(solution)/shard_map/pallas_call | solution.py:412
  36.7 0.0 collective-permute-done.8.r0
  36.7 3.8 %collective-permute-done.9.r1 = f32[5,32,128]{2,1,0:T(8,128)S(1)} collective-permute-done((f32[5,32,128]{2,1,0:T(8,128)S(1)}, f32[5,32,128]{2,1,0:T(8,128)S(1)}, u32[]{:S(2)}, u32[]{:S(2)}) %collective-permute-start.9) | collective-permute-done | bytes 81952 | tf_op jit(solution)/shard_map/ppermute | solution.py:340
  40.5 2.3 %collective-permute-start.10 = (f32[80,128]{1,0:T(8,128)S(1)}, f32[80,128]{1,0:T(8,128)S(1)}, u32[]{:S(2)}, u32[]{:S(2)}) collective-permute-start(f32[80,128]{1,0:T(8,128)S(1)} %get-tuple-element.86), channel_id=1, source_target_pairs={{0,1},{2,3},{4,5},{6,7},{1,0},{3,2},{5,4},{7,6},{8,9},{10,11},{12,... | collective-permute-start | bytes 122888 | tf_op jit(solution)/shard_map/ppermute | solution.py:340
  42.8 2.2 %collective-permute-start.11 = (f32[80,128]{1,0:T(8,128)S(1)}, f32[80,128]{1,0:T(8,128)S(1)}, u32[]{:S(2)}, u32[]{:S(2)}) collective-permute-start(f32[80,128]{1,0:T(8,128)S(1)} %get-tuple-element.87), channel_id=1, source_target_pairs={{1,2},{3,4},{5,6},{7,0},{2,1},{4,3},{6,5},{0,7},{9,10},{11,12},{13... | collective-permute-start | bytes 122888 | tf_op jit(solution)/shard_map/ppermute | solution.py:340
  45.1 2.9 %shard_map.38 = (f32[19,16,32,128]{3,2,1,0:T(8,128)}, f32[2,5,32,128]{3,2,1,0:T(8,128)S(1)}) custom-call(f32[19,16,32,128]{3,2,1,0:T(8,128)S(1)} %get-tuple-element.80.post, f32[5,32,128]{2,1,0:T(8,128)S(1)} %collective-permute-done.8.r0, f32[5,32,128]{2,1,0:T(8,128)S(1)} %collective-permute-done.9.r1, f32[6,32,128]{2,1,0:T(8,128)S(1)} %collective-permute-done.r0.flag_x0, ...), custom_call_target="tpu_custom_call" | custom-call | flops 16777216 | bytes 4194304 | tf_op jit(solution)/shard_map/pallas_call | solution.py:419
  47.9 0.0 collective-permute-done.10.s0
  47.9 2.5 %collective-permute-done.11.s1 = f32[80,128]{1,0:T(8,128)S(1)} collective-permute-done((f32[80,128]{1,0:T(8,128)S(1)}, f32[80,128]{1,0:T(8,128)S(1)}, u32[]{:S(2)}, u32[]{:S(2)}) %collective-permute-start.11) | collective-permute-done | bytes 40992 | tf_op jit(solution)/shard_map/ppermute | solution.py:340
  50.4 1.1 %shard_map.40 = f32[19,16,32,128]{3,2,1,0:T(8,128)} custom-call(f32[19,16,32,128]{3,2,1,0:T(8,128)S(1)} %get-tuple-element.80.post, f32[2,5,32,128]{3,2,1,0:T(8,128)S(1)} %get-tuple-element.83.hx, f32[80,128]{1,0:T(8,128)S(1)} %collective-permute-done.10.s0, f32[80,128]{1,0:T(8,128)S(1)} %collective-permute-done.11.s1, ...), custom_call_target="tpu_custom_call", output_to_operand_aliasing={{}: (6, {})} | custom-call | flops 16777216 | bytes 4194304 | tf_op jit(solution)/shard_map/pallas_call | solution.py:426
  (3 shorter events, 0.1 us)
Async XLA Ops:
  0.0 6.1 %copy-start.1 = (s32[16,32,128]{2,1,0:T(8,128)S(1)}, s32[16,32,128]{2,1,0:T(8,128)}, u32[]{:S(2)}) copy-start(s32[16,32,128]{2,1,0:T(8,128)} %solid.1) | copy-start | bytes 786436
  0.0 6.1 %copy-start = (f32[19,16,32,128]{3,2,1,0:T(8,128)S(1)}, f32[19,16,32,128]{3,2,1,0:T(8,128)}, u32[]{:S(2)}) copy-start(f32[19,16,32,128]{3,2,1,0:T(8,128)} %f_ref.1) | copy-start | bytes 14942212
  1.5 6.5 %collective-permute-start = (f32[6,32,128]{2,1,0:T(8,128)S(1)}, f32[6,32,128]{2,1,0:T(8,128)S(1)}, u32[]{:S(2)}, u32[]{:S(2)}) collective-permute-start(f32[6,32,128]{2,1,0:T(8,128)S(1)} %get-tuple-element.51), channel_id=1, source_target_pairs={{0,8},{16,24},{32,40},{48,56},{64,72},{80,88},{96,104},{112,120},{... | collective-permute-start | bytes 294920 | tf_op jit(solution)/shard_map/ppermute | solution.py:340
  1.6 6.9 %collective-permute-start.1 = (f32[6,32,128]{2,1,0:T(8,128)S(1)}, f32[6,32,128]{2,1,0:T(8,128)S(1)}, u32[]{:S(2)}, u32[]{:S(2)}) collective-permute-start(f32[6,32,128]{2,1,0:T(8,128)S(1)} %get-tuple-element.52), channel_id=1, source_target_pairs={{8,16},{24,32},{40,48},{56,64},{72,80},{88,96},{104,112},{120,0},{... | collective-permute-start | bytes 294920 | tf_op jit(solution)/shard_map/ppermute | solution.py:340
  8.5 8.1 %collective-permute-start.2 = (f32[104,128]{1,0:T(8,128)S(1)}, f32[104,128]{1,0:T(8,128)S(1)}, u32[]{:S(2)}, u32[]{:S(2)}) collective-permute-start(f32[104,128]{1,0:T(8,128)S(1)} %get-tuple-element.58), channel_id=1, source_target_pairs={{0,1},{2,3},{4,5},{6,7},{1,0},{3,2},{5,4},{7,6},{8,9},{10,11},{12,... | collective-permute-start | bytes 159752 | tf_op jit(solution)/shard_map/ppermute | solution.py:340
  12.1 7.7 %collective-permute-start.3 = (f32[104,128]{1,0:T(8,128)S(1)}, f32[104,128]{1,0:T(8,128)S(1)}, u32[]{:S(2)}, u32[]{:S(2)}) collective-permute-start(f32[104,128]{1,0:T(8,128)S(1)} %get-tuple-element.59), channel_id=1, source_target_pairs={{1,2},{3,4},{5,6},{7,0},{2,1},{4,3},{6,5},{0,7},{9,10},{11,12},{13... | collective-permute-start | bytes 159752 | tf_op jit(solution)/shard_map/ppermute | solution.py:340
  20.1 3.5 %collective-permute-start.4 = (f32[5,32,128]{2,1,0:T(8,128)S(1)}, f32[5,32,128]{2,1,0:T(8,128)S(1)}, u32[]{:S(2)}, u32[]{:S(2)}) collective-permute-start(f32[5,32,128]{2,1,0:T(8,128)S(1)} %get-tuple-element.66), channel_id=1, source_target_pairs={{0,8},{16,24},{32,40},{48,56},{64,72},{80,88},{96,104},{112,120},{... | collective-permute-start | bytes 245768 | tf_op jit(solution)/shard_map/ppermute | solution.py:340
  20.2 6.1 %collective-permute-start.5 = (f32[5,32,128]{2,1,0:T(8,128)S(1)}, f32[5,32,128]{2,1,0:T(8,128)S(1)}, u32[]{:S(2)}, u32[]{:S(2)}) collective-permute-start(f32[5,32,128]{2,1,0:T(8,128)S(1)} %get-tuple-element.67), channel_id=1, source_target_pairs={{8,16},{24,32},{40,48},{56,64},{72,80},{88,96},{104,112},{120,0},{... | collective-permute-start | bytes 245768 | tf_op jit(solution)/shard_map/ppermute | solution.py:340
  26.3 6.7 %collective-permute-start.6 = (f32[80,128]{1,0:T(8,128)S(1)}, f32[80,128]{1,0:T(8,128)S(1)}, u32[]{:S(2)}, u32[]{:S(2)}) collective-permute-start(f32[80,128]{1,0:T(8,128)S(1)} %get-tuple-element.73), channel_id=1, source_target_pairs={{0,1},{2,3},{4,5},{6,7},{1,0},{3,2},{5,4},{7,6},{8,9},{10,11},{12,... | collective-permute-start | bytes 122888 | tf_op jit(solution)/shard_map/ppermute | solution.py:340
  26.4 7.7 %collective-permute-start.7 = (f32[80,128]{1,0:T(8,128)S(1)}, f32[80,128]{1,0:T(8,128)S(1)}, u32[]{:S(2)}, u32[]{:S(2)}) collective-permute-start(f32[80,128]{1,0:T(8,128)S(1)} %get-tuple-element.74), channel_id=1, source_target_pairs={{1,2},{3,4},{5,6},{7,0},{2,1},{4,3},{6,5},{0,7},{9,10},{11,12},{13... | collective-permute-start | bytes 122888 | tf_op jit(solution)/shard_map/ppermute | solution.py:340
  34.3 2.3 %collective-permute-start.8 = (f32[5,32,128]{2,1,0:T(8,128)S(1)}, f32[5,32,128]{2,1,0:T(8,128)S(1)}, u32[]{:S(2)}, u32[]{:S(2)}) collective-permute-start(f32[5,32,128]{2,1,0:T(8,128)S(1)} %get-tuple-element.81), channel_id=1, source_target_pairs={{0,8},{16,24},{32,40},{48,56},{64,72},{80,88},{96,104},{112,120},{... | collective-permute-start | bytes 245768 | tf_op jit(solution)/shard_map/ppermute | solution.py:340
  34.4 6.1 %collective-permute-start.9 = (f32[5,32,128]{2,1,0:T(8,128)S(1)}, f32[5,32,128]{2,1,0:T(8,128)S(1)}, u32[]{:S(2)}, u32[]{:S(2)}) collective-permute-start(f32[5,32,128]{2,1,0:T(8,128)S(1)} %get-tuple-element.82), channel_id=1, source_target_pairs={{8,16},{24,32},{40,48},{56,64},{72,80},{88,96},{104,112},{120,0},{... | collective-permute-start | bytes 245768 | tf_op jit(solution)/shard_map/ppermute | solution.py:340
  40.5 7.4 %collective-permute-start.10 = (f32[80,128]{1,0:T(8,128)S(1)}, f32[80,128]{1,0:T(8,128)S(1)}, u32[]{:S(2)}, u32[]{:S(2)}) collective-permute-start(f32[80,128]{1,0:T(8,128)S(1)} %get-tuple-element.86), channel_id=1, source_target_pairs={{0,1},{2,3},{4,5},{6,7},{1,0},{3,2},{5,4},{7,6},{8,9},{10,11},{12,... | collective-permute-start | bytes 122888 | tf_op jit(solution)/shard_map/ppermute | solution.py:340
  42.8 7.6 %collective-permute-start.11 = (f32[80,128]{1,0:T(8,128)S(1)}, f32[80,128]{1,0:T(8,128)S(1)}, u32[]{:S(2)}, u32[]{:S(2)}) collective-permute-start(f32[80,128]{1,0:T(8,128)S(1)} %get-tuple-element.87), channel_id=1, source_target_pairs={{1,2},{3,4},{5,6},{7,0},{2,1},{4,3},{6,5},{0,7},{9,10},{11,12},{13... | collective-permute-start | bytes 122888 | tf_op jit(solution)/shard_map/ppermute | solution.py:340
